TPU v7x, 256 devices: a whole 4x4x8 slice. The times are simulated.
256 devices in a mesh: hid: 32 (over z, y), wid: 8 (over x, core).
Axes of the slice: x: 4, y: 4, z: 8, core: 2. Of those that a mesh axis runs over, the one named last changes fastest.
Arguments:
- inputs: bfloat16 [256, 12288], P(None, 'wid'), may hold values from -6 to 6
- gate_pre: bfloat16 [256, 32768], P(None, 'hid'), may hold values from -8 to 8
- up_pre: bfloat16 [256, 32768], P(None, 'hid'), may hold values from -6 to 6
- out_grad: bfloat16 [256, 12288], P(None, 'wid'), may hold values from -6 to 6
- gate_codes: int32 [6144, 32768], P('wid', 'hid'), may hold values from 0 to 255
- up_codes: int32 [6144, 32768], P('wid', 'hid'), may hold values from 0 to 255
- down_codes: int32 [16384, 12288], P('hid', 'wid'), may hold values from 0 to 255
- gate_scale: float32 [96, 32768], P('wid', 'hid'), may hold values from 0.0010825318 to 0.0027063293
- up_scale: float32 [96, 32768], P('wid', 'hid'), may hold values from 0.0010825318 to 0.0027063293
- down_scale: float32 [256, 12288], P('hid', 'wid'), may hold values from 0.0006629126 to 0.0016572815
Outputs:
- input_grad: bfloat16 [256, 12288], P('hid', 'wid')
- gate_log_grad: float32 [96, 32768], P('wid', 'hid')
- up_log_grad: float32 [96, 32768], P('wid', 'hid')
- down_log_grad: float32 [256, 12288], P('hid', 'wid')
Inputs may be any that keep to these rules, and one draw needn't show every extreme that they name: `gate_codes`: each word holds two independent four-bit codes. `up_codes`: each word holds two independent four-bit codes. `down_codes`: each word holds two independent four-bit codes.
All inputs are finite; a program needn't handle non-finite values.
Results may differ from a plain program's by a relative error of at most 0.007.
Values may be sent and summed in bfloat16 or wider, within the bound.
A program may use at most 128 MiB of HBM per device.

v0:
```python
import jax
import jax.numpy as jnp
from jax import lax
from jax.sharding import PartitionSpec as P

HB = 4096
GROUP = 128


def from_partner(value, axis, bit):
    mask = 2**bit
    pairs = [(source, source ^ mask) for source in range(lax.axis_size(axis))]
    return lax.ppermute(value, axis, pairs)


def unpack_centred(packed):
    shifts = 4 * jnp.arange(2, dtype=jnp.int32)
    nibbles = jnp.bitwise_and(jnp.right_shift(packed[:, None, :], shifts[None, :, None]), 15)
    nibbles = nibbles.reshape(packed.shape[0] * 2, packed.shape[1])
    return (nibbles - 8).astype(jnp.float32)


def dequantize(packed, scales):
    centred = unpack_centred(packed)
    weight = (centred * jnp.repeat(scales, GROUP, axis=0)).astype(jnp.bfloat16)
    return (weight, centred)


def signs_table(extent):
    indices = jnp.arange(extent, dtype=jnp.int32)
    common_bits = jnp.bitwise_and(indices[:, None], indices[None, :])
    parity = jnp.zeros((extent, extent), jnp.int32)
    for bit_index in range(extent.bit_length() - 1):
        parity = parity + jnp.bitwise_and(jnp.right_shift(common_bits, bit_index), 1)
    return (1 - 2 * (parity % 2)).astype(jnp.bfloat16)


def group_sum(values, centred, scales):
    height, across = values.shape
    return scales * (centred * values).reshape(height // GROUP, GROUP, across).sum(axis=1)


def shards(
    inputs,
    gate_pre,
    up_pre,
    out_grad,
    gate_codes,
    up_codes,
    down_codes,
    gate_scale,
    up_scale,
    down_scale,
):
    hid_width = gate_pre.shape[1]
    gate_weight, gate_centred = dequantize(gate_codes, gate_scale)
    up_weight, up_centred = dequantize(up_codes, up_scale)
    down_weight, down_centred = dequantize(down_codes, down_scale)
    partial_value = lax.dot_general(
        out_grad, down_weight, (((1,), (1,)), ((), ())), preferred_element_type=jnp.float32
    )
    summed = lax.psum(partial_value, "wid")
    rotated_grad = summed.astype(jnp.bfloat16)
    gate_val = gate_pre.astype(jnp.float32)
    up_val = up_pre.astype(jnp.float32)
    activated = jax.nn.silu(gate_val)
    hidden = (activated * up_val).astype(jnp.bfloat16)
    signs = signs_table(hid_width)
    turn_fwd = jnp.dot(hidden, signs, preferred_element_type=jnp.float32)
    turn_back = jnp.dot(rotated_grad, signs, preferred_element_type=jnp.float32)
    position = lax.axis_index("hid")
    for bit_index in range((HB // hid_width).bit_length() - 1):
        far_fwd, far_back = from_partner((turn_fwd, turn_back), "hid", bit_index)
        upper_half = jnp.bitwise_and(jnp.right_shift(position, bit_index), 1) == 1
        turn_fwd = jnp.where(upper_half, far_fwd - turn_fwd, turn_fwd + far_fwd)
        turn_back = jnp.where(upper_half, far_back - turn_back, turn_back + far_back)
    scaling = HB ** (-0.5)
    rotated = (turn_fwd * scaling).astype(jnp.bfloat16)
    hidden_grad = turn_back * scaling
    sigmoid_gate = jax.nn.sigmoid(gate_val)
    slope = sigmoid_gate * (1.0 + gate_val * (1.0 - sigmoid_gate))
    gate_grad = (hidden_grad * up_val * slope).astype(jnp.bfloat16)
    up_grad = (hidden_grad * activated).astype(jnp.bfloat16)
    contract = (((1,), (1,)), ((), ()))
    first_term = lax.dot_general(
        gate_grad, gate_weight, contract, preferred_element_type=jnp.float32
    )
    grad_inputs = lax.psum_scatter(
        first_term
        + lax.dot_general(up_grad, up_weight, contract, preferred_element_type=jnp.float32),
        "hid",
        scatter_dimension=0,
        tiled=True,
    ).astype(jnp.bfloat16)
    token_contract = (((0,), (0,)), ((), ()))
    gate_full = lax.dot_general(
        inputs, gate_grad, token_contract, preferred_element_type=jnp.float32
    )
    gate_log_grad = group_sum(gate_full, gate_centred, gate_scale)
    up_full = lax.dot_general(inputs, up_grad, token_contract, preferred_element_type=jnp.float32)
    up_log_grad = group_sum(up_full, up_centred, up_scale)
    down_full = lax.dot_general(
        rotated, out_grad, token_contract, preferred_element_type=jnp.float32
    )
    down_log_grad = group_sum(down_full, down_centred, down_scale)
    return (grad_inputs, gate_log_grad, up_log_grad, down_log_grad)


def solution(mesh):
    in_specs = (
        P(None, "wid"),
        P(None, "hid"),
        P(None, "hid"),
        P(None, "wid"),
        P("wid", "hid"),
        P("wid", "hid"),
        P("hid", "wid"),
        P("wid", "hid"),
        P("wid", "hid"),
        P("hid", "wid"),
    )
    out_specs = (P("hid", "wid"), P("wid", "hid"), P("wid", "hid"), P("hid", "wid"))
    return jax.shard_map(shards, mesh=mesh, in_specs=in_specs, out_specs=out_specs, check_vma=False)
```

profile of v0, /device:TPU:6, one launch (start us, length us, event | category | flops | bytes accessed | tf_op | source)
XLA Modules:
  0.0 427.3 jit_solution(3155021112805887350)
XLA Ops:
  7.4 6.8 %shift_right_arithmetic.142 = s32[512,2,1536]{2,1,0:T(2,128)} broadcast(s32[512,1536]{1,0:T(8,128)} %param.16), dimensions={0,2} | broadcast | bytes 9437184 | tf_op jit(solution)/shard_map/shift_right_arithmetic | solution.py:18
  14.3 8.4 %shift_right_arithmetic.143 = s32[1024,1536]{1,0:T(8,128)} reshape(s32[512,2,1536]{2,1,0:T(2,128)} %shift_right_arithmetic.142) | data formatting | bytes 12582912 | tf_op jit(solution)/shard_map/shift_right_arithmetic | solution.py:18
  22.7 3.6 fusion
  27.3 48.8 %all-reduce.1 = bf16[256,1024]{0,1:T(8,128)(2,1)S(1)} all-reduce(f32[256,1024]{0,1:T(8,128)S(1)} %convolution_bitcast_fusion), channel_id=1, replica_groups=mesh['hid'=32,'wid'=8] {'wid'}, use_global_device_ids=true, to_apply=%region_0.0 | all-reduce | flops 262144 | bytes 1572864 | tf_op jit(solution)/shard_map/psum | solution.py:62
  76.2 6.8 %fusion.16 = f32[256,1024]{1,0:T(8,128)S(1)} fusion(bf16[256,1024]{0,1:T(8,128)(2,1)S(1)} %all-reduce.1), kind=kOutput, calls=%fused_computation.28 | convolution fusion | flops 583008256 | bytes 1572864 | tf_op jit(solution)/shard_map/dot_general | solution.py:70
  84.7 22.1 %collective-permute-done = f32[256,1024]{1,0:T(8,128)} collective-permute-done((f32[256,1024]{1,0:T(8,128)S(1)}, f32[256,1024]{1,0:T(8,128)}, u32[]{:S(2)}, u32[]{:S(2)}) %collective-permute-start) | collective-permute-done | bytes 1048608 | tf_op jit(solution)/shard_map/ppermute | solution.py:13
  108.3 4.9 %collective-permute-start.1 = (f32[256,1024]{1,0:T(8,128)S(1)}, f32[256,1024]{1,0:T(8,128)}, u32[]{:S(2)}, u32[]{:S(2)}) collective-permute-start(f32[256,1024]{1,0:T(8,128)S(1)} %add_select_fusion.2), channel_id=1, source_target_pairs={{0,16},{8,24},{16,0},{24,8},{32,48},{40,56},{48,32},{56,40},{64,80... | collective-permute-start | bytes 3145736 | tf_op jit(solution)/shard_map/ppermute | solution.py:13
  113.2 8.7 %fusion.14 = f32[256,1024]{1,0:T(8,128)} fusion(bf16[256,1024]{1,0:T(8,128)(2,1)} %param.12, bf16[256,1024]{1,0:T(8,128)(2,1)S(1)} %copy-done.1), kind=kOutput, calls=%fused_computation.27 | convolution fusion | flops 585105408 | bytes 2097152 | tf_op jit(solution)/shard_map/dot_general | solution.py:69
  122.8 6.7 %shift_right_arithmetic.166 = s32[768,2,1024]{2,1,0:T(2,128)} broadcast(s32[768,1024]{1,0:T(8,128)} %param.14), dimensions={0,2} | broadcast | bytes 9437184 | tf_op jit(solution)/shard_map/shift_right_arithmetic | solution.py:18
  129.5 8.5 %shift_right_arithmetic.167 = s32[1536,1024]{1,0:T(8,128)} reshape(s32[768,2,1024]{2,1,0:T(2,128)} %shift_right_arithmetic.166) | data formatting | bytes 12582912 | tf_op jit(solution)/shard_map/shift_right_arithmetic | solution.py:18
  138.0 6.5 %copy.18 = s32[1536,1024]{0,1:T(8,128)} copy(s32[1536,1024]{1,0:T(8,128)} %shift_right_arithmetic.167) | data formatting | bytes 12582912 | tf_op jit(solution)/shard_map/shift_right_arithmetic | solution.py:18
  144.5 6.7 %shift_right_arithmetic.172 = s32[768,2,1024]{2,1,0:T(2,128)} broadcast(s32[768,1024]{1,0:T(8,128)} %param.15), dimensions={0,2} | broadcast | bytes 9437184 | tf_op jit(solution)/shard_map/shift_right_arithmetic | solution.py:18
  151.2 8.5 %shift_right_arithmetic.173 = s32[1536,1024]{1,0:T(8,128)} reshape(s32[768,2,1024]{2,1,0:T(2,128)} %shift_right_arithmetic.172) | data formatting | bytes 12582912 | tf_op jit(solution)/shard_map/shift_right_arithmetic | solution.py:18
  159.7 6.6 %copy.20 = s32[1536,1024]{0,1:T(8,128)} copy(s32[1536,1024]{1,0:T(8,128)} %shift_right_arithmetic.173) | data formatting | bytes 12582912 | tf_op jit(solution)/shard_map/shift_right_arithmetic | solution.py:18
  169.8 6.6 %copy.19 = f32[1536,1024]{0,1:T(8,128)} copy(f32[1536,1024]{1,0:T(8,128)} %bitcast.34) | data formatting | bytes 12582912 | tf_op jit(solution)/shard_map/reshape | solution.py:25
  179.9 6.6 %copy.21 = f32[1536,1024]{0,1:T(8,128)} copy(f32[1536,1024]{1,0:T(8,128)} %bitcast.35) | data formatting | bytes 12582912 | tf_op jit(solution)/shard_map/reshape | solution.py:25
  188.7 6.3 %fusion.5 = f32[256,1536]{1,0:T(8,128)S(1)} fusion(bf16[256,1024]{1,0:T(8,128)(2,1)S(1)} %get-tuple-element.5, f32[1536,1024]{0,1:T(8,128)} %copy.19, s32[1536,1024]{0,1:T(8,128)} %copy.18, s32[1536]{0:T(1024)S(1)} %shift_right_arithmetic.169), kind=kOutput, calls=%fused_computation.18 | convolution fusion | flops 814743552 | bytes 14686208 | tf_op jit(solution)/shard_map/dot_general | solution.py:85
  202.4 26.1 %collective-permute-done.3 = f32[256,1024]{1,0:T(8,128)S(1)} collective-permute-done((f32[256,1024]{1,0:T(8,128)S(1)}, f32[256,1024]{1,0:T(8,128)S(1)}, u32[]{:S(2)}, u32[]{:S(2)}) %collective-permute-start.3) | collective-permute-done | bytes 1048608 | tf_op jit(solution)/shard_map/ppermute | solution.py:13
  228.4 4.1 bitcast_reduce_fusion
  233.2 3.8 bitcast_multiply_fusion
  237.0 6.6 %copy.23 = f32[1536,1024]{1,0:T(8,128)} copy(f32[1536,1024]{0,1:T(8,128)} %bitcast_multiply_fusion) | data formatting | bytes 12582912 | tf_op jit(solution)/shard_map/mul | solution.py:40
  247.8 6.6 %bitcast_multiply_fusion.1 = f32[1536,1024]{0,1:T(8,128)} fusion(s32[1536,1024]{0,1:T(8,128)} %copy.18, bf16[256,1024]{1,0:T(8,128)(2,1)S(1)} %get-tuple-element.5, bf16[256,1536]{1,0:T(8,128)(2,1)S(1)} %copy-done, s32[1536]{0:T(1024)S(1)} %shift_right_arithmetic.169), kind=kOutput, calls=%fused_computation.2 | convolution fusion | flops 813170688 | bytes 13899776 | tf_op jit(solution)/shard_map/dot_general | solution.py:96
  254.4 6.6 %copy.22 = f32[1536,1024]{1,0:T(8,128)} copy(f32[1536,1024]{0,1:T(8,128)} %bitcast_multiply_fusion.1) | data formatting | bytes 12582912 | tf_op jit(solution)/shard_map/mul | solution.py:40
  265.1 153.9 %reduce-scatter.2.cloned.1.call-done = f32[8,1536]{1,0:T(8,128)} async-done(((f32[256,1536]{1,0:T(8,128)}), f32[8,1536]{1,0:T(8,128)}) %reduce-scatter.2.cloned.1.call-update) | async-done | bytes 49168 | tf_op jit(solution)/shard_map/reduce_scatter | solution.py:88
  (54 shorter events, 32.0 us)
Async XLA Ops:
  7.2 226.0 %copy-start = (bf16[256,1536]{1,0:T(8,128)(2,1)S(1)}, bf16[256,1536]{1,0:T(8,128)(2,1)}, u32[]{:S(2)}) copy-start(bf16[256,1536]{1,0:T(8,128)(2,1)} %param.10) | copy-start | bytes 2359300
  7.2 411.9 %reduce-scatter.2.cloned.1.call-start = ((), (), s32[]{:S(2)}) async-start(), calls=%async_computation.1 | async-start | bytes 1622016 | tf_op jit(solution)/shard_map/reduce_scatter | solution.py:88
  14.3 8.4 %copy-start.4 = (f32[8,1536]{1,0:T(8,128)S(1)}, f32[8,1536]{1,0:T(8,128)}, u32[]{:S(2)}) copy-start(f32[8,1536]{1,0:T(8,128)} %param.19) | copy-start | bytes 147460
  22.7 3.6 copy-start.6
  76.2 37.0 %copy-start.1 = (bf16[256,1024]{1,0:T(8,128)(2,1)S(1)}, bf16[256,1024]{1,0:T(8,128)(2,1)}, u32[]{:S(2)}) copy-start(bf16[256,1024]{1,0:T(8,128)(2,1)} %param.11) | copy-start | bytes 1572868
  83.0 23.8 %collective-permute-start = (f32[256,1024]{1,0:T(8,128)S(1)}, f32[256,1024]{1,0:T(8,128)}, u32[]{:S(2)}, u32[]{:S(2)}) collective-permute-start(f32[256,1024]{1,0:T(8,128)S(1)} %fusion.16), channel_id=1, source_target_pairs={{0,8},{8,0},{16,24},{24,16},{32,40},{40,32},{48,56},{56,48},{64,72... | collective-permute-start | bytes 3145736 | tf_op jit(solution)/shard_map/ppermute | solution.py:13
  108.3 78.3 %collective-permute-start.1 = (f32[256,1024]{1,0:T(8,128)S(1)}, f32[256,1024]{1,0:T(8,128)}, u32[]{:S(2)}, u32[]{:S(2)}) collective-permute-start(f32[256,1024]{1,0:T(8,128)S(1)} %add_select_fusion.2), channel_id=1, source_target_pairs={{0,16},{8,24},{16,0},{24,8},{32,48},{40,56},{48,32},{56,40},{64,80... | collective-permute-start | bytes 3145736 | tf_op jit(solution)/shard_map/ppermute | solution.py:13
  121.9 76.8 %collective-permute-start.2 = (f32[256,1024]{1,0:T(8,128)}, f32[256,1024]{1,0:T(8,128)}, u32[]{:S(2)}, u32[]{:S(2)}) collective-permute-start(f32[256,1024]{1,0:T(8,128)} %fusion.14), channel_id=1, source_target_pairs={{0,8},{8,0},{16,24},{24,16},{32,40},{40,32},{48,56},{56,48},{64,72... | collective-permute-start | bytes 3145736 | tf_op jit(solution)/shard_map/ppermute | solution.py:13
  159.7 6.6 %copy-start.3 = (f32[12,1024]{1,0:T(8,128)S(1)}, f32[12,1024]{1,0:T(8,128)}, u32[]{:S(2)}) copy-start(f32[12,1024]{1,0:T(8,128)} %param.17) | copy-start | bytes 147460
  169.8 6.6 %copy-start.2 = (f32[12,1024]{1,0:T(8,128)S(1)}, f32[12,1024]{1,0:T(8,128)}, u32[]{:S(2)}) copy-start(f32[12,1024]{1,0:T(8,128)} %param.18) | copy-start | bytes 147460
  186.5 8.5 %slice-start.4 = ((s8[6291456]{0:T(1024)(128)(4,1)}), s8[4194304]{0:T(1024)(128)(4,1)S(1)}, s32[]{:S(2)}) async-start(s8[6291456]{0:T(1024)(128)(4,1)} %bitcast.30), calls=%async_computation.6 | async-start | bytes 8388608
  188.7 6.3 %slice-start = ((s8[6291456]{0:T(1024)(128)(4,1)}), s8[4194304]{0:T(1024)(128)(4,1)S(1)}, s32[]{:S(2)}) async-start(s8[6291456]{0:T(1024)(128)(4,1)} %bitcast.26), calls=%async_computation.2 | async-start | bytes 8388608
  188.7 6.5 %slice-start.1 = ((s8[6291456]{0:T(1024)(128)(4,1)}), s8[2097152]{0:T(1024)(128)(4,1)S(1)}, s32[]{:S(2)}) async-start(s8[6291456]{0:T(1024)(128)(4,1)} %bitcast.26), calls=%async_computation.3 | async-start | bytes 4194304
  188.7 7.1 %slice-start.5 = ((s8[6291456]{0:T(1024)(128)(4,1)}), s8[2097152]{0:T(1024)(128)(4,1)S(1)}, s32[]{:S(2)}) async-start(s8[6291456]{0:T(1024)(128)(4,1)} %bitcast.30), calls=%async_computation.7 | async-start | bytes 4194304
  198.7 34.5 %slice-start.2 = ((s8[6291456]{0:T(1024)(128)(4,1)}), s8[4194304]{0:T(1024)(128)(4,1)S(1)}, s32[]{:S(2)}) async-start(s8[6291456]{0:T(1024)(128)(4,1)} %bitcast.28), calls=%async_computation.4 | async-start | bytes 8388608
  200.6 32.0 %copy-start.5 = (f32[8,1536]{1,0:T(8,128)S(1)}, f32[8,1536]{1,0:T(8,128)}, u32[]{:S(2)}) copy-start(f32[8,1536]{1,0:T(8,128)} %param.19) | copy-start | bytes 147460
  200.6 32.6 %slice-start.3 = ((s8[6291456]{0:T(1024)(128)(4,1)}), s8[2097152]{0:T(1024)(128)(4,1)S(1)}, s32[]{:S(2)}) async-start(s8[6291456]{0:T(1024)(128)(4,1)} %bitcast.28), calls=%async_computation.5 | async-start | bytes 4194304
  200.6 27.9 %collective-permute-start.3 = (f32[256,1024]{1,0:T(8,128)S(1)}, f32[256,1024]{1,0:T(8,128)S(1)}, u32[]{:S(2)}, u32[]{:S(2)}) collective-permute-start(f32[256,1024]{1,0:T(8,128)S(1)} %add_select_fusion.1), channel_id=1, source_target_pairs={{0,16},{8,24},{16,0},{24,8},{32,48},{40,56},{48,32},{56,40},{64,80... | collective-permute-start | bytes 3145736 | tf_op jit(solution)/shard_map/ppermute | solution.py:13
Sparse Core Ops, SparseCore 0:
  198.8 220.2 reduce-scatter.1
where the time goes:
time: 429 us; the launch traced here: 427 us
  waiting for transfers between devices  202 us (47%)
  local copies, waits for them, and re-layouts  93.4 us (22%)
  blocking collectives  48.8 us (11%)
  matrix products  40.2 us (9%)
  other arithmetic  19.4 us (5%)
  between operations  14.2 us (3%)
  starting transfers between devices  9.06 us (2%)
    reduce_scatter x1, waiting for transfers between devices, shards(): lax.psum_scatter(first_term + lax.dot_general(up_grad, up_weight, contrac...  154 us
    shift_right_arithmetic x12, local copies, waits for them, and re-layouts, unpack_centred(): jnp.right_shift(packed[:, None, :], shifts[None, :, None])  59.2 us
    psum x1, blocking collectives, shards(): summed = lax.psum(partial_value, 'wid')  48.8 us
    ppermute x4, waiting for transfers between devices, from_partner(): return lax.ppermute(value, axis, pairs)  48.2 us
    reshape x2, local copies, waits for them, and re-layouts, dequantize(): weight = (centred * jnp.repeat(scales, GROUP, axis=0)).astype(jnp.bfloat16)  13.2 us
    mul x2, local copies, waits for them, and re-layouts, group_sum(): centred * values  13.2 us
    ppermute x4, starting transfers between devices, from_partner(): return lax.ppermute(value, axis, pairs)  9.02 us
    dot_general x1, matrix products, shards(): turn_fwd = jnp.dot(hidden, signs, preferred_element_type=jnp.float32)  8.72 us
  transfers between devices with their start and end apart: 5, of which 3 were waited for; matrix products, arithmetic and copies ran while one was open for 29% of the time, Pallas kernels for 0%

commit v1 on v0

--- a/solution.py
+++ b/solution.py
@@ -59,7 +59,8 @@
     partial_value = lax.dot_general(
         out_grad, down_weight, (((1,), (1,)), ((), ())), preferred_element_type=jnp.float32
     )
-    summed = lax.psum(partial_value, "wid")
+    pieces = lax.all_gather(partial_value, "wid", axis=0, tiled=False)
+    summed = pieces.sum(axis=0)
     rotated_grad = summed.astype(jnp.bfloat16)
     gate_val = gate_pre.astype(jnp.float32)
     up_val = up_pre.astype(jnp.float32)

time: 429 us -> 448 us (1.044)
  waiting for transfers between devices: 202 us -> 256 us
  blocking collectives: 48.8 us -> 0 us
  local copies, waits for them, and re-layouts: 93.4 us -> 100 us
    all_gather x0 -> x1, waiting for transfers between devices: none -> 53.1 us  [shards(): pieces = lax.all_gather(partial_value, 'wid', axis=0, tiled=False)]
    psum x1 -> x0, blocking collectives: 48.8 us -> none  [shards(): summed = lax.psum(partial_value, 'wid')]
    unnamed x26 -> x27, local copies, waits for them, and re-layouts: 0.84 us -> 8.33 us
  transfers between devices with their start and end apart: 5 -> 6, of which waited for: 3 -> 4; matrix products, arithmetic and copies ran while one was open for 29% -> 28% of each run, Pallas kernels for 0% -> 0%
where the time goes in v1:
time: 448 us; the launch traced here: 443 us
  waiting for transfers between devices  256 us (57%)
  local copies, waits for them, and re-layouts  100 us (22%)
  matrix products  41.2 us (9%)
  other arithmetic  21.9 us (5%)
  between operations  14.4 us (3%)
  starting transfers between devices  8.93 us (2%)
    reduce_scatter x1, waiting for transfers between devices, shards(): lax.psum_scatter(first_term + lax.dot_general(up_grad, up_weight, contrac...  155 us
    shift_right_arithmetic x12, local copies, waits for them, and re-layouts, unpack_centred(): jnp.right_shift(packed[:, None, :], shifts[None, :, None])  59 us
    all_gather x1, waiting for transfers between devices, shards(): pieces = lax.all_gather(partial_value, 'wid', axis=0, tiled=False)  53.1 us
    ppermute x4, waiting for transfers between devices, from_partner(): return lax.ppermute(value, axis, pairs)  47.8 us
    reshape x2, local copies, waits for them, and re-layouts, dequantize(): weight = (centred * jnp.repeat(scales, GROUP, axis=0)).astype(jnp.bfloat16)  13.2 us
    mul x2, local copies, waits for them, and re-layouts, group_sum(): centred * values  13.2 us
  transfers between devices with their start and end apart: 6, of which 4 were waited for; matrix products, arithmetic and copies ran while one was open for 28% of the time, Pallas kernels for 0%

profile of v1, /device:TPU:6, one launch (start us, length us, event | category | flops | bytes accessed | tf_op | source)
XLA Modules:
  0.0 442.9 jit_solution(15619510519711244035)
XLA Ops:
  7.4 6.8 %shift_right_arithmetic.142 = s32[512,2,1536]{2,1,0:T(2,128)} broadcast(s32[512,1536]{1,0:T(8,128)} %param.16), dimensions={0,2} | broadcast | bytes 9437184 | tf_op jit(solution)/shard_map/shift_right_arithmetic | solution.py:18
  14.2 8.4 %shift_right_arithmetic.143 = s32[1024,1536]{1,0:T(8,128)} reshape(s32[512,2,1536]{2,1,0:T(2,128)} %shift_right_arithmetic.142) | data formatting | bytes 12582912 | tf_op jit(solution)/shard_map/shift_right_arithmetic | solution.py:18
  22.6 3.6 fusion
  28.6 53.1 %all-gather.3.cloned.1.call-done = f32[2048,1024]{0,1:T(8,128)} async-done(((f32[256,1024]{0,1:T(8,128)}), f32[2048,1024]{0,1:T(8,128)}) %all-gather.3.cloned.1.call-update) | async-done | bytes 8388624 | tf_op jit(solution)/shard_map/all_gather | solution.py:62
  81.7 7.5 %copy.30 = f32[128,8,8,256]{3,2,1,0:T(8,128)S(1)} copy(f32[128,8,8,256]{3,1,2,0:T(8,128)} %bitcast.41) | data formatting | bytes 16777216
  91.8 6.8 %fusion.16 = f32[256,1024]{1,0:T(8,128)S(1)} fusion(bf16[256,1024]{0,1:T(8,128)(2,1)S(1)} %bitcast_reduce_fusion), kind=kOutput, calls=%fused_computation.29 | convolution fusion | flops 583008256 | bytes 1572864 | tf_op jit(solution)/shard_map/dot_general | solution.py:71
  100.3 23.8 %collective-permute-done = f32[256,1024]{1,0:T(8,128)} collective-permute-done((f32[256,1024]{1,0:T(8,128)S(1)}, f32[256,1024]{1,0:T(8,128)}, u32[]{:S(2)}, u32[]{:S(2)}) %collective-permute-start) | collective-permute-done | bytes 1048608 | tf_op jit(solution)/shard_map/ppermute | solution.py:13
  129.0 8.7 %fusion.14 = f32[256,1024]{1,0:T(8,128)} fusion(bf16[256,1024]{1,0:T(8,128)(2,1)} %param.12, bf16[256,1024]{1,0:T(8,128)(2,1)S(1)} %copy-done.1), kind=kOutput, calls=%fused_computation.28 | convolution fusion | flops 585105408 | bytes 2097152 | tf_op jit(solution)/shard_map/dot_general | solution.py:70
  139.1 6.6 %shift_right_arithmetic.166 = s32[768,2,1024]{2,1,0:T(2,128)} broadcast(s32[768,1024]{1,0:T(8,128)} %param.14), dimensions={0,2} | broadcast | bytes 9437184 | tf_op jit(solution)/shard_map/shift_right_arithmetic | solution.py:18
  145.7 8.5 %shift_right_arithmetic.167 = s32[1536,1024]{1,0:T(8,128)} reshape(s32[768,2,1024]{2,1,0:T(2,128)} %shift_right_arithmetic.166) | data formatting | bytes 12582912 | tf_op jit(solution)/shard_map/shift_right_arithmetic | solution.py:18
  154.2 6.6 %copy.24 = s32[1536,1024]{0,1:T(8,128)} copy(s32[1536,1024]{1,0:T(8,128)} %shift_right_arithmetic.167) | data formatting | bytes 12582912 | tf_op jit(solution)/shard_map/shift_right_arithmetic | solution.py:18
  160.8 6.6 %shift_right_arithmetic.172 = s32[768,2,1024]{2,1,0:T(2,128)} broadcast(s32[768,1024]{1,0:T(8,128)} %param.15), dimensions={0,2} | broadcast | bytes 9437184 | tf_op jit(solution)/shard_map/shift_right_arithmetic | solution.py:18
  167.4 8.4 %shift_right_arithmetic.173 = s32[1536,1024]{1,0:T(8,128)} reshape(s32[768,2,1024]{2,1,0:T(2,128)} %shift_right_arithmetic.172) | data formatting | bytes 12582912 | tf_op jit(solution)/shard_map/shift_right_arithmetic | solution.py:18
  175.9 6.6 %copy.26 = s32[1536,1024]{0,1:T(8,128)} copy(s32[1536,1024]{1,0:T(8,128)} %shift_right_arithmetic.173) | data formatting | bytes 12582912 | tf_op jit(solution)/shard_map/shift_right_arithmetic | solution.py:18
  185.9 6.6 %copy.25 = f32[1536,1024]{0,1:T(8,128)} copy(f32[1536,1024]{1,0:T(8,128)} %bitcast.39) | data formatting | bytes 12582912 | tf_op jit(solution)/shard_map/reshape | solution.py:25
  195.9 6.5 %copy.27 = f32[1536,1024]{0,1:T(8,128)} copy(f32[1536,1024]{1,0:T(8,128)} %bitcast.40) | data formatting | bytes 12582912 | tf_op jit(solution)/shard_map/reshape | solution.py:25
  204.6 6.3 %fusion.5 = f32[256,1536]{1,0:T(8,128)S(1)} fusion(bf16[256,1024]{1,0:T(8,128)(2,1)S(1)} %get-tuple-element.5, f32[1536,1024]{0,1:T(8,128)} %copy.25, s32[1536,1024]{0,1:T(8,128)} %copy.24, s32[1536]{0:T(1024)S(1)} %shift_right_arithmetic.169), kind=kOutput, calls=%fused_computation.19 | convolution fusion | flops 814743552 | bytes 14686208 | tf_op jit(solution)/shard_map/dot_general | solution.py:86
  218.8 24.0 %collective-permute-done.3 = f32[256,1024]{1,0:T(8,128)S(1)} collective-permute-done((f32[256,1024]{1,0:T(8,128)S(1)}, f32[256,1024]{1,0:T(8,128)S(1)}, u32[]{:S(2)}, u32[]{:S(2)}) %collective-permute-start.3) | collective-permute-done | bytes 1048608 | tf_op jit(solution)/shard_map/ppermute | solution.py:13
  242.8 4.1 bitcast_reduce_fusion.1
  247.5 3.8 bitcast_multiply_fusion
  251.4 6.6 %copy.29 = f32[1536,1024]{1,0:T(8,128)} copy(f32[1536,1024]{0,1:T(8,128)} %bitcast_multiply_fusion) | data formatting | bytes 12582912 | tf_op jit(solution)/shard_map/mul | solution.py:40
  262.1 6.6 %bitcast_multiply_fusion.1 = f32[1536,1024]{0,1:T(8,128)} fusion(s32[1536,1024]{0,1:T(8,128)} %copy.24, bf16[256,1024]{1,0:T(8,128)(2,1)S(1)} %get-tuple-element.5, bf16[256,1536]{1,0:T(8,128)(2,1)S(1)} %copy-done, s32[1536]{0:T(1024)S(1)} %shift_right_arithmetic.169), kind=kOutput, calls=%fused_computation.3 | convolution fusion | flops 813170688 | bytes 13899776 | tf_op jit(solution)/shard_map/dot_general | solution.py:97
  268.8 6.6 %copy.28 = f32[1536,1024]{1,0:T(8,128)} copy(f32[1536,1024]{0,1:T(8,128)} %bitcast_multiply_fusion.1) | data formatting | bytes 12582912 | tf_op jit(solution)/shard_map/mul | solution.py:40
  279.5 155.0 %reduce-scatter.2.cloned.1.call-done = f32[8,1536]{1,0:T(8,128)} async-done(((f32[256,1536]{1,0:T(8,128)}), f32[8,1536]{1,0:T(8,128)}) %reduce-scatter.2.cloned.1.call-update) | async-done | bytes 49168 | tf_op jit(solution)/shard_map/reduce_scatter | solution.py:89
  (58 shorter events, 40.2 us)
Async XLA Ops:
  7.2 240.4 %copy-start = (bf16[256,1536]{1,0:T(8,128)(2,1)S(1)}, bf16[256,1536]{1,0:T(8,128)(2,1)}, u32[]{:S(2)}) copy-start(bf16[256,1536]{1,0:T(8,128)(2,1)} %param.10) | copy-start | bytes 2359300
  7.2 74.5 %all-gather.3.cloned.1.call-start = ((), (), s32[]{:S(2)}) async-start(), calls=%async_computation.2 | async-start | bytes 9437184 | tf_op jit(solution)/shard_map/all_gather | solution.py:62
  14.2 8.4 %copy-start.4 = (f32[8,1536]{1,0:T(8,128)S(1)}, f32[8,1536]{1,0:T(8,128)}, u32[]{:S(2)}) copy-start(f32[8,1536]{1,0:T(8,128)} %param.19) | copy-start | bytes 147460
  22.6 3.6 copy-start.6
  28.3 406.2 %reduce-scatter.2.cloned.1.call-start = ((), (), s32[]{:S(2)}) async-start(), calls=%async_computation.1 | async-start | bytes 1622016 | tf_op jit(solution)/shard_map/reduce_scatter | solution.py:89
  91.7 37.3 %copy-start.1 = (bf16[256,1024]{1,0:T(8,128)(2,1)S(1)}, bf16[256,1024]{1,0:T(8,128)(2,1)}, u32[]{:S(2)}) copy-start(bf16[256,1024]{1,0:T(8,128)(2,1)} %param.11) | copy-start | bytes 1572868
  98.6 25.5 %collective-permute-start = (f32[256,1024]{1,0:T(8,128)S(1)}, f32[256,1024]{1,0:T(8,128)}, u32[]{:S(2)}, u32[]{:S(2)}) collective-permute-start(f32[256,1024]{1,0:T(8,128)S(1)} %fusion.16), channel_id=1, source_target_pairs={{0,8},{8,0},{16,24},{24,16},{32,40},{40,32},{48,56},{56,48},{64,72... | collective-permute-start | bytes 3145736 | tf_op jit(solution)/shard_map/ppermute | solution.py:13
  125.5 76.9 %collective-permute-start.1 = (f32[256,1024]{1,0:T(8,128)S(1)}, f32[256,1024]{1,0:T(8,128)}, u32[]{:S(2)}, u32[]{:S(2)}) collective-permute-start(f32[256,1024]{1,0:T(8,128)S(1)} %add_select_fusion.2), channel_id=1, source_target_pairs={{0,16},{8,24},{16,0},{24,8},{32,48},{40,56},{48,32},{56,40},{64,80... | collective-permute-start | bytes 3145736 | tf_op jit(solution)/shard_map/ppermute | solution.py:13
  137.8 76.8 %collective-permute-start.2 = (f32[256,1024]{1,0:T(8,128)}, f32[256,1024]{1,0:T(8,128)}, u32[]{:S(2)}, u32[]{:S(2)}) collective-permute-start(f32[256,1024]{1,0:T(8,128)} %fusion.14), channel_id=1, source_target_pairs={{0,8},{8,0},{16,24},{24,16},{32,40},{40,32},{48,56},{56,48},{64,72... | collective-permute-start | bytes 3145736 | tf_op jit(solution)/shard_map/ppermute | solution.py:13
  175.9 6.6 %copy-start.3 = (f32[12,1024]{1,0:T(8,128)S(1)}, f32[12,1024]{1,0:T(8,128)}, u32[]{:S(2)}) copy-start(f32[12,1024]{1,0:T(8,128)} %param.17) | copy-start | bytes 147460
  185.8 6.7 %copy-start.2 = (f32[12,1024]{1,0:T(8,128)S(1)}, f32[12,1024]{1,0:T(8,128)}, u32[]{:S(2)}) copy-start(f32[12,1024]{1,0:T(8,128)} %param.18) | copy-start | bytes 147460
  202.4 8.5 %slice-start.4 = ((s8[6291456]{0:T(1024)(128)(4,1)}), s8[4194304]{0:T(1024)(128)(4,1)S(1)}, s32[]{:S(2)}) async-start(s8[6291456]{0:T(1024)(128)(4,1)} %bitcast.35), calls=%async_computation.7 | async-start | bytes 8388608
  204.6 6.3 %slice-start = ((s8[6291456]{0:T(1024)(128)(4,1)}), s8[4194304]{0:T(1024)(128)(4,1)S(1)}, s32[]{:S(2)}) async-start(s8[6291456]{0:T(1024)(128)(4,1)} %bitcast.31), calls=%async_computation.3 | async-start | bytes 8388608
  204.6 6.5 %slice-start.1 = ((s8[6291456]{0:T(1024)(128)(4,1)}), s8[2097152]{0:T(1024)(128)(4,1)S(1)}, s32[]{:S(2)}) async-start(s8[6291456]{0:T(1024)(128)(4,1)} %bitcast.31), calls=%async_computation.4 | async-start | bytes 4194304
  204.6 7.1 %slice-start.5 = ((s8[6291456]{0:T(1024)(128)(4,1)}), s8[2097152]{0:T(1024)(128)(4,1)S(1)}, s32[]{:S(2)}) async-start(s8[6291456]{0:T(1024)(128)(4,1)} %bitcast.35), calls=%async_computation.8 | async-start | bytes 4194304
  214.6 33.0 %slice-start.2 = ((s8[6291456]{0:T(1024)(128)(4,1)}), s8[4194304]{0:T(1024)(128)(4,1)S(1)}, s32[]{:S(2)}) async-start(s8[6291456]{0:T(1024)(128)(4,1)} %bitcast.33), calls=%async_computation.5 | async-start | bytes 8388608
  216.5 30.4 %copy-start.5 = (f32[8,1536]{1,0:T(8,128)S(1)}, f32[8,1536]{1,0:T(8,128)}, u32[]{:S(2)}) copy-start(f32[8,1536]{1,0:T(8,128)} %param.19) | copy-start | bytes 147460
  216.5 31.1 %slice-start.3 = ((s8[6291456]{0:T(1024)(128)(4,1)}), s8[2097152]{0:T(1024)(128)(4,1)S(1)}, s32[]{:S(2)}) async-start(s8[6291456]{0:T(1024)(128)(4,1)} %bitcast.33), calls=%async_computation.6 | async-start | bytes 4194304
  216.5 26.3 %collective-permute-start.3 = (f32[256,1024]{1,0:T(8,128)S(1)}, f32[256,1024]{1,0:T(8,128)S(1)}, u32[]{:S(2)}, u32[]{:S(2)}) collective-permute-start(f32[256,1024]{1,0:T(8,128)S(1)} %add_select_fusion.1), channel_id=1, source_target_pairs={{0,16},{8,24},{16,0},{24,8},{32,48},{40,56},{48,32},{56,40},{64,80... | collective-permute-start | bytes 3145736 | tf_op jit(solution)/shard_map/ppermute | solution.py:13
Sparse Core Ops, SparseCore 0:
  28.4 53.2 all-gather.2
  214.7 219.7 reduce-scatter.1
